TPU v7x, 32 devices: a whole 2x2x4 slice. The times are simulated.
32 devices in a mesh: groups: 2 (over y), seq: 4 (over z), inner: 2 (over x), head: 2 (over core).
Axes of the slice: x: 2, y: 2, z: 4, core: 2. Of those that a mesh axis runs over, the one named last changes fastest.
Arguments:
- queries: bfloat16 [2048, 32, 128], P(('groups', 'seq', 'inner'), 'head'), parts along dimension 0, as said below
- keys: bfloat16 [2048, 4, 128], P(('groups', 'seq', 'inner'), 'head'), parts along dimension 0
- values: bfloat16 [2048, 4, 128], P(('groups', 'seq', 'inner'), 'head'), parts along dimension 0, may hold values from -6 to 6
- log_decay: float32 [2048, 4], P(('groups', 'seq', 'inner'), 'head'), parts along dimension 0, as said below
- gain: float32 [32, 128], P('head'), may hold values from 0.1 to 1.9
- block_list: int32 [32, 16], P(('groups', 'seq', 'inner')), parts along dimension 0, may hold values from 0 to 15, as said below
Outputs:
- attended: bfloat16 [2048, 32, 128], P(('groups', 'seq', 'inner'), 'head'), parts along dimension 0
There are 2 independent parts, one for each index of `groups`. A program takes and returns all parts, laid end to end along the dimension named above; an argument that names none is the same for every part. Nothing has to cross between parts.
Inputs may be any that keep to these rules, and one draw needn't show every extreme that they name: Keys lie within -6 to 6; queries within -144 to 144. `log_decay`: each entry is below 0. `block_list`: entry 0 of row b is b. The sequence's pieces of 128 tokens fall into segments: piece p belongs to segment p modulo 2. Every entry of row b is a block at or before b in a piece of b's segment.
All inputs are finite; a program needn't handle non-finite values.
Results may differ from a plain program's by a relative error of at most 0.0017.
Values may be sent and summed in bfloat16 or wider, within the bound.
A program may use at most 64 MiB of HBM per device.

v0:
```python
import jax
import jax.numpy as jnp
from jax import lax
from jax.sharding import PartitionSpec as P

BLK = 64
SEL = 16
HIGH = lax.Precision.HIGHEST


def prefix(shard, axis, combine, identity):
    devices, here = (lax.axis_size(axis), lax.axis_index(axis))
    everything = jax.tree.map(lambda part: lax.all_gather(part, axis), shard)
    start = jax.tree.map(
        lambda part, zero: jnp.broadcast_to(jnp.asarray(zero, part.dtype), part.shape),
        shard,
        identity,
    )

    def turn(k, before):
        reached = k < here
        new = combine(before, jax.tree.map(lambda part: part[k], everything))
        return jax.tree.map(lambda a, b: jnp.where(reached, a, b), new, before)

    return lax.fori_loop(0, devices, turn, start)


def combine(earlier, later):
    return (earlier[0] * later[0], later[0][:, None, None] * earlier[1] + later[1])


def shards(queries, keys, values, log_decay, gain, block_list):
    tokens, heads_loc, width = queries.shape
    kv_loc = keys.shape[1]
    rep = heads_loc // kv_loc
    qf = queries.astype(jnp.float32).reshape(tokens, kv_loc, rep, width)
    kf = keys.astype(jnp.float32)
    vf = values.astype(jnp.float32)
    cum = jnp.cumsum(log_decay, axis=0)
    total = cum[-1]
    causal = jnp.arange(tokens)[:, None] >= jnp.arange(tokens)[None, :]
    scores = jnp.einsum("tkrd,skd->krts", qf, kf, precision=HIGH)
    diff = cum.T[:, :, None] - cum.T[:, None, :]
    weight = jnp.where(causal[None], jnp.exp(jnp.minimum(diff, 0.0)), 0.0)
    intra = jnp.einsum("krts,skd->tkrd", scores * weight[:, None], vf, precision=HIGH)
    tail = jnp.exp(total[None, :] - cum)
    own_state = jnp.einsum("skd,ske->kde", kf * tail[:, :, None], vf, precision=HIGH)
    own_decay = jnp.exp(total)
    identity = (jnp.ones_like(own_decay), jnp.zeros_like(own_state))
    prior = prefix((own_decay, own_state), ("seq", "inner"), combine, identity)
    prior_state = prior[1]
    inter = jnp.exp(cum)[:, :, None, None] * jnp.einsum(
        "tkrd,kde->tkre", qf, prior_state, precision=HIGH
    )
    linear = (intra + inter).reshape(tokens, heads_loc, width)
    normed = (
        linear * lax.rsqrt(jnp.mean(linear * linear, axis=-1, keepdims=True) + 1e-06) * gain[None]
    )
    per_piece = tokens // BLK
    n_inner = lax.axis_size("inner")
    start_pos = (lax.axis_index("seq") * n_inner + lax.axis_index("inner")) * tokens
    seg_block = block_list // (n_inner * per_piece) * per_piece + block_list % per_piece
    seg_keys, seg_values = (
        lax.all_gather(keys, "seq", axis=0, tiled=True),
        lax.all_gather(values, "seq", axis=0, tiled=True),
    )
    key_blocks = seg_keys.reshape(-1, BLK, kv_loc, width)
    value_blocks = seg_values.reshape(-1, BLK, kv_loc, width)
    picked_keys = key_blocks[seg_block]
    picked_values = value_blocks[seg_block]
    lower = jnp.arange(SEL)[None, :] < jnp.arange(SEL)[:, None]
    repeat = jnp.any((block_list[:, :, None] == block_list[:, None, :]) & lower[None], axis=2)
    keep_all = jnp.logical_not(repeat)
    query_pos = start_pos + jnp.arange(tokens).reshape(per_piece, BLK)
    key_pos = block_list[:, :, None] * BLK + jnp.arange(BLK)[None, None, :]
    q_blocks = queries.reshape(per_piece, BLK, kv_loc, rep, width)

    def one_block(args):
        qblk, pk, pv, qpos, kpos, keep = args
        valid = keep[None, :, None] & (kpos[None] <= qpos[:, None, None])
        score = jnp.einsum(
            "qkrd,jukd->krqju", qblk, pk, preferred_element_type=jnp.float32
        ) * width ** (-0.5)
        score = jnp.where(valid[None, None], score, -1e30)
        top = jnp.max(score, axis=(3, 4), keepdims=True)
        expo = jnp.where(valid[None, None], jnp.exp(score - top), 0.0)
        denom = jnp.sum(expo, axis=(3, 4))
        weights = expo.astype(jnp.bfloat16)
        out = jnp.einsum("krqju,jukd->qkrd", weights, pv, preferred_element_type=jnp.float32)
        return out / jnp.transpose(denom, (2, 0, 1))[:, :, :, None]

    outs = lax.map(one_block, (q_blocks, picked_keys, picked_values, query_pos, key_pos, keep_all))
    sparse = outs.reshape(tokens, heads_loc, width)
    return (normed + sparse).astype(jnp.bfloat16)


def solution(mesh):
    return jax.shard_map(
        shards,
        mesh=mesh,
        in_specs=(
            P(("groups", "seq", "inner"), "head", None),
            P(("groups", "seq", "inner"), "head", None),
            P(("groups", "seq", "inner"), "head", None),
            P(("groups", "seq", "inner"), "head"),
            P("head", None),
            P(("groups", "seq", "inner"), None),
        ),
        out_specs=P(("groups", "seq", "inner"), "head", None),
        check_vma=False,
    )
```

profile of v0, /device:TPU:0, one launch (start us, length us, event | category | flops | bytes accessed | tf_op | source)
XLA Modules:
  0.0 109.6 jit_solution(16745564901405145584)
XLA Ops:
  8.1 1.0 convert_multiply_fusion
  9.2 1.8 %fusion.30 = f32[2,128,128]{2,1,0:T(8,128)} fusion(f32[128,2,128]{2,1,0:T(2,128)S(1)} %convert_multiply_fusion, bf16[128,2,128]{2,1,0:T(2,128)(2,1)} %param.12), kind=kOutput, calls=%fused_computation.44 | convolution fusion | flops 50331648 | bytes 327680 | tf_op jit(solution)/shard_map/skd,ske->kde/dot_general | solution.py:47
  12.7 16.1 %all_gather.19 = bf16[512,2,128]{2,0,1:T(8,128)(2,1)S(1)} all-gather(bf16[128,2,128]{2,0,1:T(8,128)(2,1)S(1)} %copy.121), channel_id=1, replica_groups=mesh['groups'=2,'seq'=4,'inner'=2,'head'=2] {'seq'}, dimensions={0}, use_global_device_ids=true | all-gather | bytes 327680 | tf_op jit(solution)/shard_map/all_gather | solution.py:65
  31.8 15.7 %all_gather.20 = bf16[512,2,128]{2,0,1:T(8,128)(2,1)S(1)} all-gather(bf16[128,2,128]{2,0,1:T(8,128)(2,1)S(1)} %copy.129), channel_id=1, replica_groups=mesh['groups'=2,'seq'=4,'inner'=2,'head'=2] {'seq'}, dimensions={0}, use_global_device_ids=true | all-gather | bytes 327680 | tf_op jit(solution)/shard_map/all_gather | solution.py:64
  49.2 18.8 %while.24 = (s32[]{:T(128)}, f32[2,64,2,8,128]{4,3,2,1,0:T(8,128)S(1)}, bf16[2,16,64,2,128]{4,2,3,1,0:T(8,128)(2,1)S(1)}, pred[2,16]{1,0:T(4,128)(4,1)}, s32[2,1...) while((s32[]{:T(128)}, ...), condition=%wide.region_8.9_spmd, body=%wide.region_5.8_spmd.sunk | while | flops 550762496 | bytes 18383788 | solution.py:92
  51.8 1.8 %fusion.49 = (f32[2,8,64]{2,1,0:T(8,128)S(1)}, f32[2,16,64,64,8]{3,2,4,1,0:T(8,128)S(1)}) fusion(pred[64,16,64]{0,2,1:T(8,128)(4,1)S(1)} %compare_and_fusion.2, bf16[1,64,2,8,128]{4,3,2,1,0:T(8,128)(2,1)S(1)} %constant_dynamic-slice_fusion.7, bf16[1,16,64,2,128]{4,2,3,1,0:T(8,128)(2,1)S(1)} %get-tuple-element.348), kind=kOutput, calls=%fused_computation.4.clone.1 | convolution fusion | flops 271580160 | bytes 5050368 | tf_op jit(solution)/shard_map/while/body/eval_jaxpr/qkrd,jukd->krqju/dot_general | solution.py:81
  53.6 2.3 %fusion.50 = f32[2,8,64]{2,1,0:T(8,128)S(1)} fusion(f32[2,16,64,64,8]{3,2,4,1,0:T(8,128)S(1)} %get-tuple-element.349, f32[2,8,64]{2,1,0:T(8,128)S(1)} %get-tuple-element.350, pred[64,16,64]{0,2,1:T(8,128)(4,1)S(1)} %compare_and_fusion.2), kind=kLoop, calls=%fused_computation.5.clone.1 | loop fusion | flops 5241856 | bytes 4268032 | tf_op jit(solution)/shard_map/while/body/eval_jaxpr/reduce_sum | solution.py:87
  55.9 2.3 %fusion.51 = f32[1,64,2,8,128]{4,1,3,2,0:T(8,128)S(1)} fusion(f32[2,16,64,64,8]{3,2,4,1,0:T(8,128)S(1)} %get-tuple-element.349, f32[2,8,64]{2,1,0:T(8,128)S(1)} %get-tuple-element.350, pred[64,16,64]{0,2,1:T(8,128)(4,1)S(1)} %compare_and_fusion.2, bf16[1,16,64,2,128]{4,2,3,1,0:T(8,128)(2,1)S(1)} %get-tuple-element.351, f32[64,2,8]{0,2,1:T(8,128)S(1)} %bitcast.148), kind=kOutput, calls=%fused_computation.11.clone.1 | convolution fusion | flops 273809408 | bytes 5316608 | tf_op jit(solution)/shard_map/while/body/eval_jaxpr/krqju,jukd->qkrd/dot_general | solution.py:89
  61.2 1.8 %fusion.49 = (f32[2,8,64]{2,1,0:T(8,128)S(1)}, f32[2,16,64,64,8]{3,2,4,1,0:T(8,128)S(1)}) fusion(pred[64,16,64]{0,2,1:T(8,128)(4,1)S(1)} %compare_and_fusion.2, bf16[1,64,2,8,128]{4,3,2,1,0:T(8,128)(2,1)S(1)} %constant_dynamic-slice_fusion.7, bf16[1,16,64,2,128]{4,2,3,1,0:T(8,128)(2,1)S(1)} %get-tuple-element.348), kind=kOutput, calls=%fused_computation.4.clone.1 | convolution fusion | flops 271580160 | bytes 5050368 | tf_op jit(solution)/shard_map/while/body/eval_jaxpr/qkrd,jukd->krqju/dot_general | solution.py:81
  63.0 2.3 %fusion.50 = f32[2,8,64]{2,1,0:T(8,128)S(1)} fusion(f32[2,16,64,64,8]{3,2,4,1,0:T(8,128)S(1)} %get-tuple-element.349, f32[2,8,64]{2,1,0:T(8,128)S(1)} %get-tuple-element.350, pred[64,16,64]{0,2,1:T(8,128)(4,1)S(1)} %compare_and_fusion.2), kind=kLoop, calls=%fused_computation.5.clone.1 | loop fusion | flops 5241856 | bytes 4268032 | tf_op jit(solution)/shard_map/while/body/eval_jaxpr/reduce_sum | solution.py:87
  65.3 2.3 %fusion.51 = f32[1,64,2,8,128]{4,1,3,2,0:T(8,128)S(1)} fusion(f32[2,16,64,64,8]{3,2,4,1,0:T(8,128)S(1)} %get-tuple-element.349, f32[2,8,64]{2,1,0:T(8,128)S(1)} %get-tuple-element.350, pred[64,16,64]{0,2,1:T(8,128)(4,1)S(1)} %compare_and_fusion.2, bf16[1,16,64,2,128]{4,2,3,1,0:T(8,128)(2,1)S(1)} %get-tuple-element.351, f32[64,2,8]{0,2,1:T(8,128)S(1)} %bitcast.148), kind=kOutput, calls=%fused_computation.11.clone.1 | convolution fusion | flops 273809408 | bytes 5316608 | tf_op jit(solution)/shard_map/while/body/eval_jaxpr/krqju,jukd->qkrd/dot_general | solution.py:89
  68.0 20.6 %all-gather.1 = f32[8,1,2]{2,1,0:T(1,128)S(1)} all-gather(f32[1,1,2]{2,1,0:T(1,128)S(1)} %copy-done.4), channel_id=1, replica_groups=mesh['groups'=2,'seq'=4,'inner'=2,'head'=2] {'seq','inner'}, dimensions={0}, use_global_device_ids=true | all-gather | bytes 72 | tf_op jit(solution)/shard_map/all_gather | solution.py:13
  88.9 1.4 %fusion.26 = f32[2,8,128,128]{2,3,1,0:T(8,128)S(1)} fusion(f32[2,128,128]{1,2,0:T(8,128)S(1)} %exponential_select_fusion.1, bf16[128,2,8,128]{3,2,1,0:T(8,128)(2,1)} %bitcast.138, bf16[128,2,128,1]{2,1,0,3:T(2,128)(2,1)S(1)} %bitcast.144), kind=kOutput, calls=%fused_computation.38 | convolution fusion | flops 67371008 | bytes 1769472 | tf_op jit(solution)/shard_map/tkrd,skd->krts/dot_general | solution.py:42
  91.0 8.3 %while.25 = (s32[]{:T(128)}, f32[2,128,128]{2,1,0:T(8,128)S(1)}, s32[]{:T(128)}, f32[8,2]{1,0:T(8,128)S(1)}, f32[8,2,128,128]{3,2,1,0:T(8,128)}, /*index=5*/s32[]{:T(128)}, s32[]{:T(128)}) while((s32[]{:T(128)}, f32[2,128,128]{2,1,0:T(8,128)S(1)}, s32[]{:T(128)}, f32[8,2]{1,0:T(8,128)S(1)}, f32[8,2,128,128]{3,2,1,0:T(8,128)}, ...), condition=%wide.region_2.3_spmd.clone, body=%wide.region_1.2_spmd.clone.sunk | while | flops 131076 | bytes 393353 | solution.py:25
  91.0 1.0 fusion.52
  92.0 1.0 fusion.52
  93.1 1.0 fusion.52
  94.1 1.0 fusion.52
  95.1 1.0 fusion.52
  96.2 1.0 fusion.52
  97.2 1.0 fusion.52
  98.2 1.0 fusion.52
  99.2 1.8 %multiply_reduce_fusion = (f32[128,2,8]{0,2,1:T(8,128)S(1)}, f32[128,2,8,128]{0,3,2,1:T(8,128)S(1)}) fusion(f32[128,2,8,128]{0,3,2,1:T(8,128)S(1)} %convolution_bitcast_fusion.2, bf16[128,2,8,128]{3,2,1,0:T(8,128)(2,1)} %bitcast.139, f32[2,128,128]{2,1,0:T(8,128)S(1)} %get-tuple-element.141, f32[128,2]{0,1:T(2,128)S(1)} %copy.118), kind=kOutput, calls=%fused_computation.40 | convolution fusion | flops 403699712 | bytes 2761728 | tf_op jit(solution)/shard_map/tkrd,kde->tkre/dot_general | solution.py:52
  101.6 1.1 %add_convert_fusion = bf16[128,16,128]{2,1,0:T(8,128)(2,1)} fusion(f32[128,16,128]{2,1,0:T(8,128)S(1)} %bitcast.143, f32[128,16,128]{2,1,0:T(8,128)S(1)} %copy.126, f32[16,128]{1,0:T(8,128)S(1)} %copy-done.3, f32[128,16]{1,0:T(8,128)S(1)} %copy.125), kind=kLoop, calls=%fused_computation.39 | loop fusion | flops 1048576 | bytes 2637824 | tf_op jit(solution)/shard_map/convert_element_type | solution.py:94
  (63 shorter events, 15.6 us)
Async XLA Ops:
  6.5 84.4 %all-gather.4.cloned.1.call-start = ((), (), s32[]{:S(2)}) async-start(), calls=%async_computation | async-start | bytes 1179648 | tf_op jit(solution)/shard_map/all_gather | solution.py:13
  29.6 17.9 %copy-start.2 = (s32[1024]{0:T(1024)}, s32[1024]{0:T(1024)S(1)}, u32[]{:S(2)}) copy-start(s32[1024]{0:T(1024)S(1)} %pad_clamp_fusion) | copy-start | bytes 12292
  49.1 18.8 %copy-start.4 = (f32[1,1,2]{2,1,0:T(1,128)S(1)}, f32[1,1,2]{2,1,0:T(1,128)}, u32[]{:S(2)}) copy-start(f32[1,1,2]{2,1,0:T(1,128)} %get-tuple-element.264) | copy-start | bytes 28
  49.1 39.7 %copy-start = (bf16[128,2,128]{2,1,0:T(2,128)(2,1)S(1)}, bf16[128,2,128]{2,1,0:T(2,128)(2,1)}, u32[]{:S(2)}) copy-start(bf16[128,2,128]{2,1,0:T(2,128)(2,1)} %param.11) | copy-start | bytes 196612
  49.2 41.1 %copy-start.1 = (bf16[128,2,128]{2,1,0:T(2,128)(2,1)S(1)}, bf16[128,2,128]{2,1,0:T(2,128)(2,1)}, u32[]{:S(2)}) copy-start(bf16[128,2,128]{2,1,0:T(2,128)(2,1)} %param.12) | copy-start | bytes 196612
  67.9 33.7 %copy-start.3 = (f32[16,128]{1,0:T(8,128)S(1)}, f32[16,128]{1,0:T(8,128)}, u32[]{:S(2)}) copy-start(f32[16,128]{1,0:T(8,128)} %param.14) | copy-start | bytes 24580
Sparse Core Ops, SparseCore 0:
  11.1 43.3 all-gather.3
where the time goes:
time: 110 us
  blocking collectives  52.4 us (48%)
  other arithmetic  18.3 us (17%)
  matrix products  13.7 us (12%)
  between operations  13.6 us (12%)
  local copies, waits for them, and re-layouts  11.2 us (10%)
    all_gather x1, blocking collectives, prefix(): everything = jax.tree.map(lambda part: lax.all_gather(part, axis), shard)  20.6 us
    all_gather x1, blocking collectives, shards(): lax.all_gather(values, 'seq', axis=0, tiled=True)  16.1 us
    all_gather x1, blocking collectives, shards(): lax.all_gather(keys, 'seq', axis=0, tiled=True)  15.7 us
    select_n x8, other arithmetic, turn(): return jax.tree.map(lambda a, b: jnp.where(reached, a, b), new, before)  7.94 us
    dot_general x2, matrix products, one_block(): jnp.einsum('krqju,jukd->qkrd', weights, pv, preferred_element_type=jnp.fl...  4.6 us
    reduce_sum x2, other arithmetic, one_block(): denom = jnp.sum(expo, axis=(3, 4))  4.54 us
    dot_general x2, matrix products, one_block(): jnp.einsum('qkrd,jukd->krqju', qblk, pk, preferred_element_type=jnp.float32)  3.54 us
    unnamed x13, local copies, waits for them, and re-layouts  2.52 us
  transfers between devices with their start and end apart: 1, of which 0 were waited for; matrix products, arithmetic and copies ran while one was open for 25% of the time, Pallas kernels for 0%

commit v1 on v0

--- a/solution.py
+++ b/solution.py
@@ -6,6 +6,18 @@
 BLK = 64
 SEL = 16
 HIGH = lax.Precision.HIGHEST
+
+
+def ring_gather(shard, axis, dim):
+    ways, here, step = (lax.axis_size(axis), lax.axis_index(axis), shard.shape[dim])
+    shape = [n * ways if d == dim else n for d, n in enumerate(shard.shape)]
+    full = lax.dynamic_update_slice_in_dim(
+        jnp.zeros(shape, shard.dtype), shard, here * step, axis=dim
+    )
+    for far in range(1, ways):
+        shard = lax.ppermute(shard, axis, [(d, (d + 1) % ways) for d in range(ways)])
+        full = lax.dynamic_update_slice_in_dim(full, shard, (here - far) % ways * step, axis=dim)
+    return full
 
 
 def prefix(shard, axis, combine, identity):
@@ -61,7 +73,7 @@
     start_pos = (lax.axis_index("seq") * n_inner + lax.axis_index("inner")) * tokens
     seg_block = block_list // (n_inner * per_piece) * per_piece + block_list % per_piece
     seg_keys, seg_values = (
-        lax.all_gather(keys, "seq", axis=0, tiled=True),
+        ring_gather(keys, "seq", 0),
         lax.all_gather(values, "seq", axis=0, tiled=True),
     )
     key_blocks = seg_keys.reshape(-1, BLK, kv_loc, width)

time: 110 us -> 106 us (0.964)
  blocking collectives: 52.4 us -> 34.2 us
  waiting for transfers between devices: 0.04 us -> 12.1 us
  local copies, waits for them, and re-layouts: 11.2 us -> 7.58 us
  starting transfers between devices: 0.01 us -> 3.17 us
  matrix products: 13.7 us -> 15.8 us
    all_gather x1 -> x0, blocking collectives: 15.7 us -> none  [shards(): lax.all_gather(keys, 'seq', axis=0, tiled=True)]
    ppermute x0 -> x3, waiting for transfers between devices: none -> 12.1 us  [ring_gather(): lax.ppermute(shard, axis, [(d, (d + 1) % ways) for d in range(ways)])]
    ppermute x0 -> x3, starting transfers between devices: none -> 3.17 us  [ring_gather(): lax.ppermute(shard, axis, [(d, (d + 1) % ways) for d in range(ways)])]
    all_gather x1, blocking collectives: 20.6 us -> 18.5 us  [prefix(): everything = jax.tree.map(lambda part: lax.all_gather(part, axis), shard)]
    dynamic_slice x4, local copies, waits for them, and re-layouts: 2.11 us -> 0.21 us  [shards(): lax.map(one_block, (q_blocks, picked_keys, picked_values, query_pos, key_...]
    dot_general x1, matrix products: 0.68 us -> 2.54 us  [shards(): jnp.einsum('krts,skd->tkrd', scores * weight[:, None], vf, precision=HIGH)]
    dynamic_update_slice x2, local copies, waits for them, and re-layouts: 0.7 us -> 2.21 us  [shards(): lax.map(one_block, (q_blocks, picked_keys, picked_values, query_pos, key_...]
    le x4, local copies, waits for them, and re-layouts: 1.38 us -> 0.02 us  [one_block(): valid = keep[None, :, None] & (kpos[None] <= qpos[:, None, None])]
  transfers between devices with their start and end apart: 1 -> 4, of which waited for: 0 -> 2; matrix products, arithmetic and copies ran while one was open for 25% -> 26% of each run, Pallas kernels for 0% -> 0%
where the time goes in v1:
time: 106 us; the launch traced here: 105 us
  blocking collectives  34.2 us (32%)
  other arithmetic  18.4 us (17%)
  matrix products  15.8 us (15%)
  between operations  13.6 us (13%)
  waiting for transfers between devices  12.1 us (11%)
  local copies, waits for them, and re-layouts  7.58 us (7%)
  starting transfers between devices  3.17 us (3%)
    all_gather x1, blocking collectives, prefix(): everything = jax.tree.map(lambda part: lax.all_gather(part, axis), shard)  18.5 us
    all_gather x1, blocking collectives, shards(): lax.all_gather(values, 'seq', axis=0, tiled=True)  15.7 us
    ppermute x3, waiting for transfers between devices, ring_gather(): lax.ppermute(shard, axis, [(d, (d + 1) % ways) for d in range(ways)])  12.1 us
    select_n x8, other arithmetic, turn(): return jax.tree.map(lambda a, b: jnp.where(reached, a, b), new, before)  7.94 us
    dot_general x2, matrix products, one_block(): jnp.einsum('krqju,jukd->qkrd', weights, pv, preferred_element_type=jnp.fl...  4.55 us
    reduce_sum x2, other arithmetic, one_block(): denom = jnp.sum(expo, axis=(3, 4))  4.53 us
    dot_general x2, matrix products, one_block(): jnp.einsum('qkrd,jukd->krqju', qblk, pk, preferred_element_type=jnp.float32)  3.54 us
    ppermute x3, starting transfers between devices, ring_gather(): lax.ppermute(shard, axis, [(d, (d + 1) % ways) for d in range(ways)])  3.17 us
  transfers between devices with their start and end apart: 4, of which 2 were waited for; matrix products, arithmetic and copies ran while one was open for 26% of the time, Pallas kernels for 0%

profile of v1, /device:TPU:0, one launch (start us, length us, event | category | flops | bytes accessed | tf_op | source)
XLA Modules:
  0.0 105.1 jit_solution(10155431566955906545)
XLA Ops:
  7.5 3.1 %collective-permute-start = (bf16[128,2,128]{2,0,1:T(8,128)(2,1)S(1)}, bf16[128,2,128]{2,0,1:T(8,128)(2,1)S(1)}, u32[]{:S(2)}, u32[]{:S(2)}) collective-permute-start(bf16[128,2,128]{2,0,1:T(8,128)(2,1)S(1)} %get-tuple-element.265), channel_id=1, source_target_pairs={{0,4},{4,8},{8,12},{12,0},{1,5},{5,9},{9,13},{13,1},{2,6},{6,10},{... | collective-permute-start | bytes 196616 | tf_op jit(solution)/shard_map/ppermute | solution.py:18
  11.6 1.0 convert_multiply_fusion
  12.7 1.8 %fusion.30 = f32[2,128,128]{2,1,0:T(8,128)} fusion(f32[128,2,128]{2,1,0:T(2,128)S(1)} %convert_multiply_fusion, bf16[128,2,128]{2,1,0:T(2,128)(2,1)} %param.12), kind=kOutput, calls=%fused_computation.44 | convolution fusion | flops 50331648 | bytes 327680 | tf_op jit(solution)/shard_map/skd,ske->kde/dot_general | solution.py:59
  16.2 15.7 %all_gather.16 = bf16[512,2,128]{2,0,1:T(8,128)(2,1)S(1)} all-gather(bf16[128,2,128]{2,0,1:T(8,128)(2,1)S(1)} %copy.123), channel_id=1, replica_groups=mesh['groups'=2,'seq'=4,'inner'=2,'head'=2] {'seq'}, dimensions={0}, use_global_device_ids=true | all-gather | bytes 327680 | tf_op jit(solution)/shard_map/all_gather | solution.py:77
  32.9 18.5 %all-gather.1 = f32[8,1,2]{2,1,0:T(1,128)S(1)} all-gather(f32[1,1,2]{2,1,0:T(1,128)S(1)} %get-tuple-element.264), channel_id=1, replica_groups=mesh['groups'=2,'seq'=4,'inner'=2,'head'=2] {'seq','inner'}, dimensions={0}, use_global_device_ids=true | all-gather | bytes 72 | tf_op jit(solution)/shard_map/all_gather | solution.py:25
  52.5 1.4 %fusion.26 = f32[2,8,128,128]{2,3,1,0:T(8,128)S(1)} fusion(f32[2,128,128]{1,2,0:T(8,128)S(1)} %exponential_select_fusion.1, bf16[128,2,8,128]{3,2,1,0:T(8,128)(2,1)} %bitcast.137, bf16[128,2,128,1]{2,1,0,3:T(2,128)(2,1)} %bitcast.143), kind=kOutput, calls=%fused_computation.38 | convolution fusion | flops 67371008 | bytes 1769472 | tf_op jit(solution)/shard_map/tkrd,skd->krts/dot_general | solution.py:54
  53.9 2.5 %convolution_bitcast_fusion.2 = f32[128,2,8,128]{0,3,2,1:T(8,128)} fusion(f32[2,8,128,128]{2,3,1,0:T(8,128)S(1)} %fusion.26, bf16[128,2,128,1]{2,1,0,3:T(2,128)(2,1)} %bitcast.144), kind=kOutput, calls=%fused_computation.37 | convolution fusion | flops 402653184 | bytes 2162688 | tf_op jit(solution)/shard_map/krts,skd->tkrd/dot_general | solution.py:57
  56.5 6.0 %collective-permute-done.1 = bf16[128,2,128]{2,0,1:T(8,128)(2,1)S(1)} collective-permute-done((bf16[128,2,128]{2,0,1:T(8,128)(2,1)S(1)}, bf16[128,2,128]{2,0,1:T(8,128)(2,1)S(1)}, u32[]{:S(2)}, u32[]{:S(2)}) %collective-permute-start.1) | collective-permute-done | bytes 65568 | tf_op jit(solution)/shard_map/ppermute | solution.py:18
  62.6 6.0 %collective-permute-done.2 = bf16[128,2,128]{2,0,1:T(8,128)(2,1)S(1)} collective-permute-done((bf16[128,2,128]{2,0,1:T(8,128)(2,1)S(1)}, bf16[128,2,128]{2,0,1:T(8,128)(2,1)S(1)}, u32[]{:S(2)}, u32[]{:S(2)}) %collective-permute-start.2) | collective-permute-done | bytes 65568 | tf_op jit(solution)/shard_map/ppermute | solution.py:18
  69.4 15.7 %while.24 = (s32[]{:T(128)}, f32[2,64,2,8,128]{4,3,2,1,0:T(8,128)}, bf16[2,16,64,2,128]{4,2,3,1,0:T(8,128)(2,1)S(1)}, pred[2,16]{1,0:T(4,128)(4,1)S(1)}, s32[2,1...) while((s32[]{:T(128)}, f32[2,64,2,8,128]{4,3,2,1,0:T(8,128)}, ...), condition=%wide.region_8.9_spmd, body=%wide.region_5.8_spmd.sunk | while | flops 550762496 | bytes 18384288 | solution.py:104
  69.9 1.8 %fusion.50 = (f32[2,8,64]{2,1,0:T(8,128)S(1)}, f32[2,16,64,64,8]{3,2,4,1,0:T(8,128)S(1)}) fusion(pred[64,16,64]{0,2,1:T(8,128)(4,1)S(1)} %compare_and_fusion.2, bf16[1,64,2,8,128]{4,3,2,1,0:T(8,128)(2,1)S(1)} %constant_dynamic-slice_fusion.7, bf16[1,16,64,2,128]{4,2,3,1,0:T(8,128)(2,1)S(1)} %get-tuple-element.350), kind=kOutput, calls=%fused_computation.4.clone.1 | convolution fusion | flops 271580160 | bytes 5050368 | tf_op jit(solution)/shard_map/while/body/eval_jaxpr/qkrd,jukd->krqju/dot_general | solution.py:93
  71.6 2.3 %fusion.51 = f32[2,8,64]{2,1,0:T(8,128)S(1)} fusion(f32[2,16,64,64,8]{3,2,4,1,0:T(8,128)S(1)} %get-tuple-element.351, f32[2,8,64]{2,1,0:T(8,128)S(1)} %get-tuple-element.352, pred[64,16,64]{0,2,1:T(8,128)(4,1)S(1)} %compare_and_fusion.2), kind=kLoop, calls=%fused_computation.5.clone.1 | loop fusion | flops 5241856 | bytes 4268032 | tf_op jit(solution)/shard_map/while/body/eval_jaxpr/reduce_sum | solution.py:99
  73.9 2.3 %fusion.52 = f32[1,64,2,8,128]{4,1,3,2,0:T(8,128)S(1)} fusion(f32[2,16,64,64,8]{3,2,4,1,0:T(8,128)S(1)} %get-tuple-element.351, f32[2,8,64]{2,1,0:T(8,128)S(1)} %get-tuple-element.352, pred[64,16,64]{0,2,1:T(8,128)(4,1)S(1)} %compare_and_fusion.2, bf16[1,16,64,2,128]{4,2,3,1,0:T(8,128)(2,1)S(1)} %get-tuple-element.353, f32[64,2,8]{0,2,1:T(8,128)S(1)} %bitcast.147), kind=kOutput, calls=%fused_computation.11.clone.1 | convolution fusion | flops 273809408 | bytes 5316608 | tf_op jit(solution)/shard_map/while/body/eval_jaxpr/krqju,jukd->qkrd/dot_general | solution.py:101
  76.2 1.1 %copy_dynamic-update-slice_fusion.2 = f32[2,64,2,8,128]{4,3,2,1,0:T(8,128)} fusion(f32[2,64,2,8,128]{4,3,2,1,0:T(8,128)} %get-tuple-element.369, s32[]{:T(128)} %get-tuple-element.368, f32[1,64,2,8,128]{4,1,3,2,0:T(8,128)S(1)} %fusion.52), kind=kLoop, calls=%fused_computation.13.clone.1 | loop fusion | bytes 1049088 | tf_op jit(solution)/shard_map/while/body/jit(dynamic_update_index_in_dim)/dynamic_update_slice | solution.py:104
  77.7 1.8 %fusion.50 = (f32[2,8,64]{2,1,0:T(8,128)S(1)}, f32[2,16,64,64,8]{3,2,4,1,0:T(8,128)S(1)}) fusion(pred[64,16,64]{0,2,1:T(8,128)(4,1)S(1)} %compare_and_fusion.2, bf16[1,64,2,8,128]{4,3,2,1,0:T(8,128)(2,1)S(1)} %constant_dynamic-slice_fusion.7, bf16[1,16,64,2,128]{4,2,3,1,0:T(8,128)(2,1)S(1)} %get-tuple-element.350), kind=kOutput, calls=%fused_computation.4.clone.1 | convolution fusion | flops 271580160 | bytes 5050368 | tf_op jit(solution)/shard_map/while/body/eval_jaxpr/qkrd,jukd->krqju/dot_general | solution.py:93
  79.4 2.3 %fusion.51 = f32[2,8,64]{2,1,0:T(8,128)S(1)} fusion(f32[2,16,64,64,8]{3,2,4,1,0:T(8,128)S(1)} %get-tuple-element.351, f32[2,8,64]{2,1,0:T(8,128)S(1)} %get-tuple-element.352, pred[64,16,64]{0,2,1:T(8,128)(4,1)S(1)} %compare_and_fusion.2), kind=kLoop, calls=%fused_computation.5.clone.1 | loop fusion | flops 5241856 | bytes 4268032 | tf_op jit(solution)/shard_map/while/body/eval_jaxpr/reduce_sum | solution.py:99
  81.7 2.3 %fusion.52 = f32[1,64,2,8,128]{4,1,3,2,0:T(8,128)S(1)} fusion(f32[2,16,64,64,8]{3,2,4,1,0:T(8,128)S(1)} %get-tuple-element.351, f32[2,8,64]{2,1,0:T(8,128)S(1)} %get-tuple-element.352, pred[64,16,64]{0,2,1:T(8,128)(4,1)S(1)} %compare_and_fusion.2, bf16[1,16,64,2,128]{4,2,3,1,0:T(8,128)(2,1)S(1)} %get-tuple-element.353, f32[64,2,8]{0,2,1:T(8,128)S(1)} %bitcast.147), kind=kOutput, calls=%fused_computation.11.clone.1 | convolution fusion | flops 273809408 | bytes 5316608 | tf_op jit(solution)/shard_map/while/body/eval_jaxpr/krqju,jukd->qkrd/dot_general | solution.py:101
  84.0 1.1 %copy_dynamic-update-slice_fusion.2 = f32[2,64,2,8,128]{4,3,2,1,0:T(8,128)} fusion(f32[2,64,2,8,128]{4,3,2,1,0:T(8,128)} %get-tuple-element.369, s32[]{:T(128)} %get-tuple-element.368, f32[1,64,2,8,128]{4,1,3,2,0:T(8,128)S(1)} %fusion.52), kind=kLoop, calls=%fused_computation.13.clone.1 | loop fusion | bytes 1049088 | tf_op jit(solution)/shard_map/while/body/jit(dynamic_update_index_in_dim)/dynamic_update_slice | solution.py:104
  85.1 8.2 %while.25 = (s32[]{:T(128)}, f32[2,128,128]{2,1,0:T(8,128)S(1)}, s32[]{:T(128)}, f32[8,2]{1,0:T(8,128)S(1)}, f32[8,2,128,128]{3,2,1,0:T(8,128)}, /*index=5*/s32[]{:T(128)}, s32[]{:T(128)}) while((s32[]{:T(128)}, f32[2,128,128]{2,1,0:T(8,128)S(1)}, s32[]{:T(128)}, f32[8,2]{1,0:T(8,128)S(1)}, f32[8,2,128,128]{3,2,1,0:T(8,128)}, ...), condition=%wide.region_2.3_spmd.clone, body=%wide.region_1.2_spmd.clone.sunk | while | flops 131076 | bytes 393345 | solution.py:37
  85.1 1.0 fusion.53
  86.2 1.0 fusion.53
  87.2 1.0 fusion.53
  93.4 1.9 %multiply_reduce_fusion = (f32[128,2,8]{0,2,1:T(8,128)S(1)}, f32[128,2,8,128]{0,3,2,1:T(8,128)S(1)}) fusion(f32[128,2,8,128]{0,3,2,1:T(8,128)} %convolution_bitcast_fusion.2, bf16[128,2,8,128]{3,2,1,0:T(8,128)(2,1)S(1)} %bitcast.139, f32[2,128,128]{2,1,0:T(8,128)S(1)} %get-tuple-element.141, f32[128,2]{0,1:T(2,128)S(1)} %copy.120), kind=kOutput, calls=%fused_computation.40 | convolution fusion | flops 403699712 | bytes 2761728 | tf_op jit(solution)/shard_map/tkrd,kde->tkre/dot_general | solution.py:64
  95.9 2.4 %add_convert_fusion = bf16[128,16,128]{2,1,0:T(8,128)(2,1)} fusion(f32[128,16,128]{2,1,0:T(8,128)} %bitcast.38, f32[128,16,128]{2,1,0:T(8,128)S(1)} %copy.128, f32[16,128]{1,0:T(8,128)S(1)} %copy-done.1, f32[128,16]{1,0:T(8,128)S(1)} %copy.127), kind=kLoop, calls=%fused_computation.39 | loop fusion | flops 1048576 | bytes 2637824 | tf_op jit(solution)/shard_map/convert_element_type | solution.py:106
  (66 shorter events, 12.9 us)
Async XLA Ops:
  6.5 62.9 %copy-start = (bf16[128,16,128]{2,1,0:T(8,128)(2,1)S(1)}, bf16[128,16,128]{2,1,0:T(8,128)(2,1)}, u32[]{:S(2)}) copy-start(bf16[128,16,128]{2,1,0:T(8,128)(2,1)} %param.10) | copy-start | bytes 1572868
  6.5 78.6 %all-gather.4.cloned.1.call-start = ((), (), s32[]{:S(2)}) async-start(), calls=%async_computation | async-start | bytes 1179648 | tf_op jit(solution)/shard_map/all_gather | solution.py:25
  7.5 48.9 %collective-permute-start = (bf16[128,2,128]{2,0,1:T(8,128)(2,1)S(1)}, bf16[128,2,128]{2,0,1:T(8,128)(2,1)S(1)}, u32[]{:S(2)}, u32[]{:S(2)}) collective-permute-start(bf16[128,2,128]{2,0,1:T(8,128)(2,1)S(1)} %get-tuple-element.265), channel_id=1, source_target_pairs={{0,4},{4,8},{8,12},{12,0},{1,5},{5,9},{9,13},{13,1},{2,6},{6,10},{... | collective-permute-start | bytes 196616 | tf_op jit(solution)/shard_map/ppermute | solution.py:18
  56.4 6.1 %collective-permute-start.1 = (bf16[128,2,128]{2,0,1:T(8,128)(2,1)S(1)}, bf16[128,2,128]{2,0,1:T(8,128)(2,1)S(1)}, u32[]{:S(2)}, u32[]{:S(2)}) collective-permute-start(bf16[128,2,128]{2,0,1:T(8,128)(2,1)S(1)} %collective-permute-done), channel_id=1, source_target_pairs={{0,4},{4,8},{8,12},{12,0},{1,5},{5,9},{9,13},{13,1},{2,6},{6,10},{... | collective-permute-start | bytes 196616 | tf_op jit(solution)/shard_map/ppermute | solution.py:18
  62.6 6.1 %collective-permute-start.2 = (bf16[128,2,128]{2,0,1:T(8,128)(2,1)S(1)}, bf16[128,2,128]{2,0,1:T(8,128)(2,1)S(1)}, u32[]{:S(2)}, u32[]{:S(2)}) collective-permute-start(bf16[128,2,128]{2,0,1:T(8,128)(2,1)S(1)} %collective-permute-done.1), channel_id=1, source_target_pairs={{0,4},{4,8},{8,12},{12,0},{1,5},{5,9},{9,13},{13,1},{2,6},{6,10},{... | collective-permute-start | bytes 196616 | tf_op jit(solution)/shard_map/ppermute | solution.py:18
  69.4 26.5 %copy-start.1 = (f32[16,128]{1,0:T(8,128)S(1)}, f32[16,128]{1,0:T(8,128)}, u32[]{:S(2)}) copy-start(f32[16,128]{1,0:T(8,128)} %param.14) | copy-start | bytes 24580
Sparse Core Ops, SparseCore 0:
  14.6 41.6 all-gather.3
